TPU v7x, 512 devices: a whole 4x8x8 slice. The times are simulated.
512 devices in a mesh: ctx: 64 (over y_hi, z, core), tp: 8 (over x, y_lo).
Axes of the slice: x: 4, y: 8 (y_hi: 4, y_lo: 2; y = y_hi * 2 + y_lo), z: 8, core: 2. Of those that a mesh axis runs over, the one named last changes fastest.
Arguments:
- q_new: bfloat16 [1024, 8192], P(('ctx', 'tp')), may hold values from -128 to 128
- kv_new: bfloat16 [2, 1024, 1024], P(None, 'ctx', 'tp'), may hold values from -4 to 4
- kv_cache: bfloat16 [2, 31744, 1024], P(None, 'ctx', 'tp'), may hold values from -4 to 4
- cache_lens: int32 [64], replicated, may hold values from 1 to 496, 15872 in all
- segment_ids: int32 [1024], replicated, may hold values from 0 to 63, never falling along the last dimension, each value on 1 to 32 neighbouring positions
Outputs:
- attn_out: bfloat16 [1024, 8192], P(('ctx', 'tp'))
- attn_lse: float32 [1024, 64], P('ctx', 'tp')
Inputs may be any that keep to these rules, and one draw needn't show every extreme that they name: The filled slots of shard c are its first cache_lens[c] slots; the lengths sum to 15872 and some shard is full. `segment_ids`: never falls along the turn; a segment holds at most 32 tokens, and some segment exactly 32.
All inputs are finite; a program needn't handle non-finite values.
Results may differ from a plain program's by a relative error of at most 0.0015.
Values may be sent and summed in bfloat16 or wider, within the bound.
No kernel may reach another device: no remote copies, remote signals or barrier semaphores. Data moves between devices by JAX's collectives and lax.ppermute only.
A program may use at most 64 MiB of HBM per device.

v0:
```python
import jax
import jax.numpy as jnp
from jax import lax
from jax.sharding import PartitionSpec as P


def shard_partial(queries, query_seg, keys_all, values_all, filled, key_seg, head_dim):
    rows = queries.shape[0]
    heads = queries.shape[1] // head_dim
    total = keys_all.shape[0]
    cache_count = total - key_seg.shape[0]
    flat = queries.reshape(rows * heads, head_dim)
    scores = lax.dot_general(
        flat, keys_all, (((1,), (1,)), ((), ())), preferred_element_type=jnp.float32
    ) * head_dim ** (-0.5)
    scores = scores.reshape(rows, heads, total)
    slot_rank = jnp.where(jnp.arange(cache_count) < filled, -1, 2**30).astype(jnp.int32)
    key_rank = jnp.concatenate([slot_rank, key_seg])
    visible = key_rank[None, None, :] <= query_seg[:, None, None]
    masked = jnp.where(visible, scores, -jnp.inf)
    peak = jnp.max(masked, axis=2)
    expo = jnp.exp(masked - peak[:, :, None])
    denom = jnp.sum(expo, axis=2)
    weights = expo.astype(jnp.bfloat16).reshape(rows * heads, total)
    mixed = jnp.dot(weights, values_all, preferred_element_type=jnp.float32)
    mixed = mixed.reshape(rows, heads, head_dim) / denom[:, :, None]
    return (mixed.reshape(rows, heads * head_dim), peak + jnp.log(denom))


def shards(q_new, kv_new, kv_cache, cache_lens, segment_ids):
    head_dim = kv_cache.shape[2]
    block = kv_new.shape[1]
    here = lax.axis_index("ctx")
    count = lax.axis_size("ctx")
    queries = lax.all_to_all(q_new, "tp", split_axis=1, concat_axis=0, tiled=True)
    heads = queries.shape[1] // head_dim
    keys_all = jnp.concatenate([kv_cache[0], kv_new[0]])
    values_all = jnp.concatenate([kv_cache[1], kv_new[1]])
    filled = cache_lens[here]
    key_seg = lax.dynamic_slice_in_dim(segment_ids, here * block, block, 0)
    total_rows = block * count
    init = (
        jnp.zeros((total_rows, heads * head_dim), jnp.float32),
        jnp.zeros((total_rows, heads), jnp.float32),
    )
    piece = lax.all_gather(queries, "ctx", axis=0, tiled=True)
    rows = piece.shape[0]
    width = 64

    def one_block(index, inner):
        outs, lses = inner
        offset = index * width
        part = lax.dynamic_slice_in_dim(piece, index * width, width, 0)
        part_seg = lax.dynamic_slice_in_dim(segment_ids, offset, width, 0)
        mixed, lse = shard_partial(part, part_seg, keys_all, values_all, filled, key_seg, head_dim)
        outs = lax.dynamic_update_slice_in_dim(outs, mixed, offset, 0)
        lses = lax.dynamic_update_slice_in_dim(lses, lse, offset, 0)
        return (outs, lses)

    partial_out, partial_lse = lax.fori_loop(0, rows // width, one_block, init)
    got_out, got_lse = (
        lax.all_to_all(
            partial_out.reshape(count, block, heads * head_dim),
            "ctx",
            split_axis=0,
            concat_axis=0,
            tiled=True,
        ),
        lax.all_to_all(
            partial_lse.reshape(count, block, heads), "ctx", split_axis=0, concat_axis=0, tiled=True
        ),
    )
    peak = jnp.max(got_lse, axis=0)
    scale = jnp.exp(got_lse - peak[None])
    denom = jnp.sum(scale, axis=0)
    numer = jnp.sum(got_out.reshape(count, block, heads, head_dim) * scale[:, :, :, None], axis=0)
    final = (numer / denom[:, :, None]).reshape(block, heads * head_dim)
    lse_out = peak + jnp.log(denom)
    attn_out = lax.all_to_all(
        final.astype(jnp.bfloat16), "tp", split_axis=0, concat_axis=1, tiled=True
    )
    return (attn_out, lse_out)


def solution(mesh):
    return jax.shard_map(
        shards,
        mesh=mesh,
        in_specs=(P(("ctx", "tp"), None), P(None, "ctx", "tp"), P(None, "ctx", "tp"), P(), P()),
        out_specs=(P(("ctx", "tp"), None), P("ctx", "tp")),
        check_vma=False,
    )
```

profile of v0, /device:TPU:272, one launch (start us, length us, event | category | flops | bytes accessed | tf_op | source)
XLA Modules:
  0.0 346.2 jit_solution(2459077010839411977)
XLA Ops:
  7.2 11.6 %all_to_all.45 = bf16[2,8,1024]{2,0,1:T(2,128)(2,1)S(1)} all-to-all(bf16[2,8,1024]{2,0,1:T(2,128)(2,1)} %bitcast.53), channel_id=1, replica_groups=mesh['ctx'=64,'tp'=8] {'tp'}, dimensions={1} | all-to-all | bytes 65536 | tf_op jit(solution)/shard_map/all_to_all | solution.py:35
  19.5 1.2 dynamic_slice.20
  22.2 1.0 slice_bitcast_fusion
  23.2 76.2 %all-gather.2.cloned.1.call-done = bf16[1024,1024]{1,0:T(8,128)(2,1)} async-done(((bf16[16,1024]{1,0:T(8,128)(2,1)}), bf16[1024,1024]{1,0:T(8,128)(2,1)}) %all-gather.2.cloned.1.call-update) | async-done | bytes 2097168 | tf_op jit(solution)/shard_map/all_gather | solution.py:46
  99.4 2.5 broadcast_in_dim.61
  102.0 74.2 %while.15 = (s32[]{:T(128)}, f32[1024,1024]{1,0:T(8,128)}, f32[1024,8]{1,0:T(8,128)S(1)}, s32[]{:T(128)}, s32[16]{0:T(128)S(1)}, /*index=5*/s32[1024]{0:T(1024)}...) while((s32[]{:T(128)}, f32[1024,1024]{1,0:T(8,128)}, ...), condition=%wide.region_3.4_spmd, body=%wide.region_0.3_spmd.sunk | while | flops 136152032 | bytes 5041031 | solution.py:60
  102.0 0.9 constant_dynamic-slice_fusion.2
  103.7 0.8 dynamic_slice.26
  105.7 0.8 bitcast_dynamic-update-slice_fusion.2
  106.6 0.9 constant_dynamic-slice_fusion.2
  108.3 0.8 dynamic_slice.26
  111.2 0.9 constant_dynamic-slice_fusion.2
  112.9 0.8 dynamic_slice.26
  115.0 0.8 bitcast_dynamic-update-slice_fusion.2
  115.9 0.9 constant_dynamic-slice_fusion.2
  117.6 0.8 dynamic_slice.26
  119.6 0.8 bitcast_dynamic-update-slice_fusion.2
  120.5 0.9 constant_dynamic-slice_fusion.2
  122.2 0.8 dynamic_slice.26
  125.2 0.9 constant_dynamic-slice_fusion.2
  128.9 0.8 bitcast_dynamic-update-slice_fusion.2
  129.8 0.9 constant_dynamic-slice_fusion.2
  131.5 0.8 dynamic_slice.26
  133.6 0.8 bitcast_dynamic-update-slice_fusion.2
  134.5 0.9 constant_dynamic-slice_fusion.2
  138.2 0.8 bitcast_dynamic-update-slice_fusion.2
  139.1 0.9 constant_dynamic-slice_fusion.2
  140.8 0.8 dynamic_slice.26
  142.9 0.8 bitcast_dynamic-update-slice_fusion.2
  143.8 0.9 constant_dynamic-slice_fusion.2
  145.5 0.8 dynamic_slice.26
  147.5 0.8 bitcast_dynamic-update-slice_fusion.2
  148.4 0.9 constant_dynamic-slice_fusion.2
  152.1 0.8 bitcast_dynamic-update-slice_fusion.2
  153.0 0.9 constant_dynamic-slice_fusion.2
  157.7 0.9 constant_dynamic-slice_fusion.2
  162.3 0.9 constant_dynamic-slice_fusion.2
  166.9 0.9 constant_dynamic-slice_fusion.2
  171.5 0.9 constant_dynamic-slice_fusion.2
  175.3 0.8 bitcast_dynamic-update-slice_fusion.2
  176.5 16.2 %all_to_all.46 = f32[64,1,128]{2,1,0:T(1,128)S(1)} all-to-all(f32[64,1,128]{2,1,0:T(1,128)S(1)} %reshape.108), channel_id=1, replica_groups=mesh['ctx'=64,'tp'=8] {'ctx'}, dimensions={0} | all-to-all | bytes 65536 | tf_op jit(solution)/shard_map/all_to_all | solution.py:69
  192.7 12.0 %all-to-all-start.1 = ((f32[64,16,1024]{2,1,0:T(8,128)}), f32[64,16,1024]{2,1,0:T(8,128)}, u32[]{:S(2)}, u32[]{:S(2)}) async-start(f32[64,16,1024]{2,1,0:T(8,128)} %bitcast.46), calls=%async_computation.1 | async-start | bytes 8388608 | tf_op jit(solution)/shard_map/all_to_all | solution.py:62
  206.9 2.6 mul.30
  209.4 4.9 %mul.31 = f32[64,16,1024]{2,1,0:T(8,128)} reshape(f32[64,16,8,128]{3,2,1,0:T(8,128)} %mul.30) | data formatting | bytes 8388608 | tf_op jit(solution)/shard_map/mul | solution.py:76
  214.5 109.1 %all-to-all-done.1 = f32[64,16,1024]{2,1,0:T(8,128)} async-done(((f32[64,16,1024]{2,1,0:T(8,128)}), f32[64,16,1024]{2,1,0:T(8,128)}, u32[]{:S(2)}, u32[]{:S(2)}) %all-to-all-start.1) | async-done | bytes 4194336 | tf_op jit(solution)/shard_map/all_to_all | solution.py:62
  323.6 4.0 %multiply_reduce_fusion = f32[16,1024]{1,0:T(8,128)S(1)} fusion(f32[64,16,1024]{2,1,0:T(8,128)} %all-to-all-done.1, f32[64,16,1024]{2,1,0:T(8,128)} %mul.31), kind=kLoop, calls=%fused_computation.16 | loop fusion | flops 2080768 | bytes 8454144 | tf_op jit(solution)/shard_map/reduce_sum | solution.py:76
  328.2 4.3 %all-to-all-start.3 = ((bf16[8,2,1024]{2,1,0:T(2,128)(2,1)}), bf16[8,2,1024]{2,1,0:T(2,128)(2,1)S(1)}, u32[]{:S(2)}, u32[]{:S(2)}) async-start(bf16[8,2,1024]{2,1,0:T(2,128)(2,1)} %divide_convert_fusion), calls=%async_computation.3 | async-start | bytes 65536 | tf_op jit(solution)/shard_map/all_to_all | solution.py:79
  333.2 5.6 %all-to-all-done.3 = bf16[8,2,1024]{2,1,0:T(2,128)(2,1)S(1)} async-done(((bf16[8,2,1024]{2,1,0:T(2,128)(2,1)}), bf16[8,2,1024]{2,1,0:T(2,128)(2,1)S(1)}, u32[]{:S(2)}, u32[]{:S(2)}) %all-to-all-start.3) | async-done | bytes 32800 | tf_op jit(solution)/shard_map/all_to_all | solution.py:79
  (198 shorter events, 51.2 us)
Async XLA Ops:
  7.2 92.2 %all-gather.2.cloned.1.call-start = ((), (), s32[]{:S(2)}) async-start(), calls=%async_computation.4 | async-start | bytes 2129920 | tf_op jit(solution)/shard_map/all_gather | solution.py:46
  192.7 130.9 %all-to-all-start.1 = ((f32[64,16,1024]{2,1,0:T(8,128)}), f32[64,16,1024]{2,1,0:T(8,128)}, u32[]{:S(2)}, u32[]{:S(2)}) async-start(f32[64,16,1024]{2,1,0:T(8,128)} %bitcast.46), calls=%async_computation.1 | async-start | bytes 8388608 | tf_op jit(solution)/shard_map/all_to_all | solution.py:62
  328.2 10.5 %all-to-all-start.3 = ((bf16[8,2,1024]{2,1,0:T(2,128)(2,1)}), bf16[8,2,1024]{2,1,0:T(2,128)(2,1)S(1)}, u32[]{:S(2)}, u32[]{:S(2)}) async-start(bf16[8,2,1024]{2,1,0:T(2,128)(2,1)} %divide_convert_fusion), calls=%async_computation.3 | async-start | bytes 65536 | tf_op jit(solution)/shard_map/all_to_all | solution.py:79
Sparse Core Ops, SparseCore 0:
  19.6 79.7 all-gather.1
where the time goes:
time: 348 us; the launch traced here: 346 us
  waiting for transfers between devices  191 us (55%)
  local copies, waits for them, and re-layouts  60.1 us (17%)
  blocking collectives  27.8 us (8%)
  other arithmetic  23.3 us (7%)
  starting transfers between devices  16.3 us (5%)
  between operations  14.1 us (4%)
  matrix products  12.4 us (4%)
    all_to_all x1, waiting for transfers between devices, shards(): lax.all_to_all(partial_out.reshape(count, block, heads * head_dim), 'ctx'...  109 us
    all_gather x1, waiting for transfers between devices, shards(): piece = lax.all_gather(queries, 'ctx', axis=0, tiled=True)  76.2 us
    all_to_all x1, blocking collectives, shards(): lax.all_to_all(partial_lse.reshape(count, block, heads), 'ctx', split_axi...  16.2 us
    dynamic_slice x16, local copies, waits for them, and re-layouts, one_block(): part = lax.dynamic_slice_in_dim(piece, index * width, width, 0)  14.7 us
    dynamic_update_slice x16, local copies, waits for them, and re-layouts, one_block(): outs = lax.dynamic_update_slice_in_dim(outs, mixed, offset, 0)  12.2 us
    dynamic_slice x16, local copies, waits for them, and re-layouts, one_block(): part_seg = lax.dynamic_slice_in_dim(segment_ids, offset, width, 0)  12.2 us
    all_to_all x1, starting transfers between devices, shards(): lax.all_to_all(partial_out.reshape(count, block, heads * head_dim), 'ctx'...  12 us
    all_to_all x1, blocking collectives, shards(): lax.all_to_all(q_new, 'tp', split_axis=1, concat_axis=0, tiled=True)  11.6 us
  transfers between devices with their start and end apart: 3, of which 3 were waited for; matrix products, arithmetic and copies ran while one was open for 4% of the time, Pallas kernels for 0%

commit v1 on v0

--- a/solution.py
+++ b/solution.py
@@ -43,7 +43,10 @@
         jnp.zeros((total_rows, heads * head_dim), jnp.float32),
         jnp.zeros((total_rows, heads), jnp.float32),
     )
-    piece = lax.all_gather(queries, "ctx", axis=0, tiled=True)
+    size = lax.axis_size("ctx")
+    blocks = jnp.stack([queries for _ in range(size)])
+    blocks = lax.all_to_all(blocks, "ctx", split_axis=0, concat_axis=0)
+    piece = jnp.concatenate(blocks, axis=0)
     rows = piece.shape[0]
     width = 64
 

time: 348 us -> 323 us (0.928)
  the two profiles are of different devices: /device:TPU:272 before, /device:TPU:288 now
where the time goes in v1:
time: 323 us; the launch traced here: 322 us
  waiting for transfers between devices  160 us (50%)
  local copies, waits for them, and re-layouts  46 us (14%)
  starting transfers between devices  42.3 us (13%)
  other arithmetic  33.4 us (10%)
  blocking collectives  26.5 us (8%)
  matrix products  12.4 us (4%)
    all_to_all x1, waiting for transfers between devices, shards(): lax.all_to_all(partial_out.reshape(count, block, heads * head_dim), 'ctx'...  107 us
    all_to_all x1, waiting for transfers between devices, shards(): blocks = lax.all_to_all(blocks, 'ctx', split_axis=0, concat_axis=0)  46.5 us
    all_to_all x1, blocking collectives, shards(): lax.all_to_all(partial_lse.reshape(count, block, heads), 'ctx', split_axi...  15.7 us
    all_to_all x1, starting transfers between devices, shards(): lax.all_to_all(partial_out.reshape(count, block, heads * head_dim), 'ctx'...  15.1 us
    all_to_all x1, starting transfers between devices, shards(): lax.all_to_all(final.astype(jnp.bfloat16), 'tp', split_axis=0, concat_axi...  14.4 us
    all_to_all x1, starting transfers between devices, shards(): blocks = lax.all_to_all(blocks, 'ctx', split_axis=0, concat_axis=0)  12.8 us
    dynamic_update_slice x16, local copies, waits for them, and re-layouts, one_block(): outs = lax.dynamic_update_slice_in_dim(outs, mixed, offset, 0)  12.2 us
    dynamic_slice x16, local copies, waits for them, and re-layouts, one_block(): part_seg = lax.dynamic_slice_in_dim(segment_ids, offset, width, 0)  12.2 us
  transfers between devices with their start and end apart: 3, of which 3 were waited for; matrix products, arithmetic and copies ran while one was open for 4% of the time, Pallas kernels for 0%

profile of v1, /device:TPU:288, one launch (start us, length us, event | category | flops | bytes accessed | tf_op | source)
XLA Modules:
  0.0 321.7 jit_solution(11147633082476388669)
XLA Ops:
  0.7 10.8 %all_to_all.47 = bf16[2,8,1024]{2,0,1:T(2,128)(2,1)S(1)} all-to-all(bf16[2,8,1024]{2,0,1:T(2,128)(2,1)} %bitcast.55), channel_id=1, replica_groups=mesh['ctx'=64,'tp'=8] {'tp'}, dimensions={1} | all-to-all | bytes 65536 | tf_op jit(solution)/shard_map/all_to_all | solution.py:35
  11.5 1.6 stack.5
  13.1 12.8 %all-to-all-start.1 = ((bf16[64,16,1024]{2,1,0:T(8,128)(2,1)}), bf16[64,16,1024]{2,1,0:T(8,128)(2,1)S(1)}, u32[]{:S(2)}, u32[]{:S(2)}) async-start(bf16[64,16,1024]{2,1,0:T(8,128)(2,1)} %stack.5), calls=%async_computation.1 | async-start | bytes 4194304 | tf_op jit(solution)/shard_map/all_to_all | solution.py:48
  26.5 0.8 dynamic_slice.21
  27.3 46.5 %all-to-all-done.1 = bf16[64,16,1024]{2,1,0:T(8,128)(2,1)S(1)} async-done(((bf16[64,16,1024]{2,1,0:T(8,128)(2,1)}), bf16[64,16,1024]{2,1,0:T(8,128)(2,1)S(1)}, u32[]{:S(2)}, u32[]{:S(2)}) %all-to-all-start.1) | async-done | bytes 2097184 | tf_op jit(solution)/shard_map/all_to_all | solution.py:48
  73.8 2.5 broadcast_in_dim.61
  76.3 0.8 broadcast_in_dim.62
  77.1 69.2 %while.15 = (s32[]{:T(128)}, f32[1024,1024]{1,0:T(8,128)}, f32[1024,8]{1,0:T(8,128)}, s32[]{:T(128)}, s32[16]{0:T(128)S(1)}, /*index=5*/s32[1024]{0:T(1024)}, bf...) while((s32[]{:T(128)}, f32[1024,1024]{1,0:T(8,128)}, ...), condition=%wide.region_3.4_spmd, body=%wide.region_0.3_spmd.sunk | while | flops 136152032 | bytes 4979591 | solution.py:63
  78.0 0.8 dynamic_slice.26
  82.3 0.8 dynamic_slice.26
  84.3 0.8 bitcast_dynamic-update-slice_fusion.2
  86.6 0.8 dynamic_slice.26
  88.6 0.8 bitcast_dynamic-update-slice_fusion.2
  90.9 0.8 dynamic_slice.26
  92.9 0.8 bitcast_dynamic-update-slice_fusion.2
  95.2 0.8 dynamic_slice.26
  97.3 0.8 bitcast_dynamic-update-slice_fusion.2
  99.6 0.8 dynamic_slice.26
  101.6 0.8 bitcast_dynamic-update-slice_fusion.2
  103.9 0.8 dynamic_slice.26
  105.9 0.8 bitcast_dynamic-update-slice_fusion.2
  108.2 0.8 dynamic_slice.26
  110.3 0.8 bitcast_dynamic-update-slice_fusion.2
  112.6 0.8 dynamic_slice.26
  114.6 0.8 bitcast_dynamic-update-slice_fusion.2
  116.9 0.8 dynamic_slice.26
  118.9 0.8 bitcast_dynamic-update-slice_fusion.2
  121.2 0.8 dynamic_slice.26
  123.3 0.8 bitcast_dynamic-update-slice_fusion.2
  125.6 0.8 dynamic_slice.26
  127.6 0.8 bitcast_dynamic-update-slice_fusion.2
  129.9 0.8 dynamic_slice.26
  131.9 0.8 bitcast_dynamic-update-slice_fusion.2
  134.2 0.8 dynamic_slice.26
  136.2 0.7 bitcast_dynamic-update-slice_fusion.2
  138.5 0.8 dynamic_slice.26
  140.6 0.8 bitcast_dynamic-update-slice_fusion.2
  142.8 0.8 dynamic_slice.26
  144.9 0.8 bitcast_dynamic-update-slice_fusion.2
  146.3 1.2 copy.28
  147.7 15.7 %all_to_all.48 = f32[64,1,128]{2,1,0:T(1,128)S(1)} all-to-all(f32[64,1,128]{2,1,0:T(1,128)S(1)} %reshape.115), channel_id=1, replica_groups=mesh['ctx'=64,'tp'=8] {'ctx'}, dimensions={0} | all-to-all | bytes 65536 | tf_op jit(solution)/shard_map/all_to_all | solution.py:72
  163.4 15.1 %all-to-all-start.2 = ((f32[64,16,1024]{2,1,0:T(8,128)}), f32[64,16,1024]{2,1,0:T(8,128)}, u32[]{:S(2)}, u32[]{:S(2)}) async-start(f32[64,16,1024]{2,1,0:T(8,128)} %bitcast.47), calls=%async_computation.2 | async-start | bytes 8388608 | tf_op jit(solution)/shard_map/all_to_all | solution.py:65
  180.7 2.6 mul.30
  183.3 4.9 %mul.31 = f32[64,16,1024]{2,1,0:T(8,128)} reshape(f32[64,16,8,128]{3,2,1,0:T(8,128)} %mul.30) | data formatting | bytes 8388608 | tf_op jit(solution)/shard_map/mul | solution.py:79
  188.3 107.4 %all-to-all-done.2 = f32[64,16,1024]{2,1,0:T(8,128)} async-done(((f32[64,16,1024]{2,1,0:T(8,128)}), f32[64,16,1024]{2,1,0:T(8,128)}, u32[]{:S(2)}, u32[]{:S(2)}) %all-to-all-start.2) | async-done | bytes 4194336 | tf_op jit(solution)/shard_map/all_to_all | solution.py:65
  295.7 4.0 %multiply_reduce_fusion = f32[16,1024]{1,0:T(8,128)S(1)} fusion(f32[64,16,1024]{2,1,0:T(8,128)} %all-to-all-done.2, f32[64,16,1024]{2,1,0:T(8,128)} %mul.31), kind=kLoop, calls=%fused_computation.16 | loop fusion | flops 2080768 | bytes 8454144 | tf_op jit(solution)/shard_map/reduce_sum | solution.py:79
  300.4 14.4 %all-to-all-start.4 = ((bf16[8,2,1024]{2,1,0:T(2,128)(2,1)}), bf16[8,2,1024]{2,1,0:T(2,128)(2,1)S(1)}, u32[]{:S(2)}, u32[]{:S(2)}) async-start(bf16[8,2,1024]{2,1,0:T(2,128)(2,1)} %divide_convert_fusion), calls=%async_computation.4 | async-start | bytes 65536 | tf_op jit(solution)/shard_map/all_to_all | solution.py:82
  315.5 5.6 %all-to-all-done.4 = bf16[8,2,1024]{2,1,0:T(2,128)(2,1)S(1)} async-done(((bf16[8,2,1024]{2,1,0:T(2,128)(2,1)}), bf16[8,2,1024]{2,1,0:T(2,128)(2,1)S(1)}, u32[]{:S(2)}, u32[]{:S(2)}) %all-to-all-start.4) | async-done | bytes 32800 | tf_op jit(solution)/shard_map/all_to_all | solution.py:82
  (204 shorter events, 49.8 us)
Async XLA Ops:
  0.6 25.2 %copy-start.2 = (s32[64]{0:T(128)S(1)}, s32[64]{0:T(128)}, u32[]{:S(2)}) copy-start(s32[64]{0:T(128)} %param.10) | copy-start | bytes 772
  0.6 26.6 %copy-start.1 = (bf16[2,16,128]{2,1,0:T(8,128)(2,1)S(1)}, bf16[2,16,128]{2,1,0:T(8,128)(2,1)}, u32[]{:S(2)}) copy-start(bf16[2,16,128]{2,1,0:T(8,128)(2,1)} %param.8) | copy-start | bytes 24580
  0.7 26.6 %copy-start = (bf16[2,496,128]{2,1,0:T(8,128)(2,1)S(1)}, bf16[2,496,128]{2,1,0:T(8,128)(2,1)}, u32[]{:S(2)}) copy-start(bf16[2,496,128]{2,1,0:T(8,128)(2,1)} %param.9) | copy-start | bytes 761860
  13.1 60.7 %all-to-all-start.1 = ((bf16[64,16,1024]{2,1,0:T(8,128)(2,1)}), bf16[64,16,1024]{2,1,0:T(8,128)(2,1)S(1)}, u32[]{:S(2)}, u32[]{:S(2)}) async-start(bf16[64,16,1024]{2,1,0:T(8,128)(2,1)} %stack.5), calls=%async_computation.1 | async-start | bytes 4194304 | tf_op jit(solution)/shard_map/all_to_all | solution.py:48
  163.4 132.3 %all-to-all-start.2 = ((f32[64,16,1024]{2,1,0:T(8,128)}), f32[64,16,1024]{2,1,0:T(8,128)}, u32[]{:S(2)}, u32[]{:S(2)}) async-start(f32[64,16,1024]{2,1,0:T(8,128)} %bitcast.47), calls=%async_computation.2 | async-start | bytes 8388608 | tf_op jit(solution)/shard_map/all_to_all | solution.py:65
  300.4 20.7 %all-to-all-start.4 = ((bf16[8,2,1024]{2,1,0:T(2,128)(2,1)}), bf16[8,2,1024]{2,1,0:T(2,128)(2,1)S(1)}, u32[]{:S(2)}, u32[]{:S(2)}) async-start(bf16[8,2,1024]{2,1,0:T(2,128)(2,1)} %divide_convert_fusion), calls=%async_computation.4 | async-start | bytes 65536 | tf_op jit(solution)/shard_map/all_to_all | solution.py:82
